TPU v7x, 32 devices: a whole 2x2x4 slice. The times are simulated.
32 devices in a mesh: wave: 8 (over z, y), lev: 4 (over x, core).
Axes of the slice: x: 2, y: 2, z: 4, core: 2. Of those that a mesh axis runs over, the one named last changes fastest.
Arguments:
- grid_data: float32 [2048, 32, 384], P('wave', None, 'lev'), may hold values from -6 to 6
- legendre: float32 [32, 1024, 1024], P('wave'), may hold values from -0.125 to 0.125
- gauss_weights: float32 [1024], replicated, may hold values from 0.4 to 2
- wave_of_slot: int32 [32], replicated, may hold values from 0 to 31, as said below
- first_tile: int32 [32], P('wave'), may hold values from 0 to 7, as said below
- coupling: float32 [64, 64], P(None, 'lev'), may hold values from -0.75 to 0.75
Outputs:
- grid_out: float32 [2048, 32, 384], P('wave', None, 'lev')
Inputs may be any that keep to these rules, and one draw needn't show every extreme that they name: `wave_of_slot`: A permutation of the waves; slots 2q and 2q + 1 hold waves j and 31 - j for some j. `first_tile`: tends to grow with the slot's wavenumber; the slot holding wave 32 - 1 has 7 and the one holding wave 0 has 0.
All inputs are finite; a program needn't handle non-finite values.
Results may differ from a plain program's by a relative error of at most 0.0003.
Values sent between devices are 32-bit elements; how exact they have to be, the bound alone decides.
A program may use at most 128 MiB of HBM per device.

v0:
```python
import functools

import jax
import jax.numpy as jnp
from jax import lax
from jax.experimental import pallas as pl
from jax.experimental.pallas import tpu as pltpu
from jax.sharding import PartitionSpec as P

TILE = 128
FIELDS = 6
PAIR = 2
FIRST = 2
MESH = pl.DeviceIdType.MESH
NN = (((1,), (0,)), ((), ()))
NT = (((1,), (1,)), ((), ()))
VMEM_BYTES = 64 * 1024 * 1000


def mm(a, b, dims=NN):
    return lax.dot_general(a, b, dims, preferred_element_type=jnp.float32)


def split(v):
    high = v.astype(jnp.bfloat16)
    return high, (v - high.astype(jnp.float32)).astype(jnp.bfloat16)


def mm3(a_high, a_low, b_high, b_low, dims=NN):
    return mm(a_high, b_high, dims) + (mm(a_low, b_high, dims) + mm(a_high, b_low, dims))


def iota(shape, axis):
    return lax.broadcasted_iota(jnp.int32, shape, axis)


def pack_kernel(wave_ref, x_ref, out_ref):
    waves = wave_ref.shape[0]
    lats = out_ref.shape[2]
    wave = wave_ref[pl.program_id(0)]
    out_ref[0] = x_ref[pl.ds(wave, lats, stride=waves), :].T


def pack(wave_of_slot, grid_data):
    lats, waves, cols = grid_data.shape
    return pl.pallas_call(
        pack_kernel,
        grid_spec=pltpu.PrefetchScalarGridSpec(
            num_scalar_prefetch=1,
            grid=(waves,),
            in_specs=[pl.BlockSpec((lats * waves, cols), lambda s, w: (0, 0))],
            out_specs=pl.BlockSpec((1, cols, lats), lambda s, w: (s, 0, 0)),
        ),
        out_shape=jax.ShapeDtypeStruct((waves, cols, lats), jnp.float32),
        compiler_params=pltpu.CompilerParams(vmem_limit_bytes=VMEM_BYTES),
        name="pack",
    )(wave_of_slot, grid_data.reshape(lats * waves, cols))


def unpack_kernel(wave_ref, y_ref, out_ref):
    waves = wave_ref.shape[0]
    lats = y_ref.shape[2]
    wave = wave_ref[pl.program_id(0)]
    out_ref[pl.ds(wave, lats, stride=waves), :] = y_ref[0].T


def unpack(wave_of_slot, packed):
    waves, cols, lats = packed.shape
    out = pl.pallas_call(
        unpack_kernel,
        grid_spec=pltpu.PrefetchScalarGridSpec(
            num_scalar_prefetch=1,
            grid=(waves,),
            in_specs=[pl.BlockSpec((1, cols, lats), lambda s, w: (s, 0, 0))],
            out_specs=pl.BlockSpec((lats * waves, cols), lambda s, w: (0, 0)),
        ),
        out_shape=jax.ShapeDtypeStruct((lats * waves, cols), jnp.float32),
        compiler_params=pltpu.CompilerParams(vmem_limit_bytes=VMEM_BYTES),
        name="unpack",
    )(wave_of_slot, packed)
    return out.reshape(lats, waves, cols)


def spectral_kernel(
    W, NL,
    wave_ref, tile_ref, gauss_ref, coupling_ref, packed_ref, tables_ref, out_ref,
    tab, recv, osend, lev_send, lev_recv, x_high, x_low, spec, r_high, r_low, k_high, k_low,
    tab_sem, own_sem, in_send, in_recv, lev_ssem, lev_rsem, out_own, out_send, out_recv,
):
    SL, H, N = tab.shape
    C, LAT = recv.shape[2], recv.shape[3]
    waves = wave_ref.shape[0]
    LP = C // FIELDS
    half = W // 2
    TW = max(256, LAT)
    BPT = TW // LAT
    nt = H // TW
    NW = 256
    me = lax.axis_index("wave")
    ml = lax.axis_index("lev")
    order = sorted(range(1, W), key=lambda d: (abs(d - half), d))
    lev_order = sorted(range(1, NL), key=lambda d: (abs(d - NL // 2), d))

    barrier = pltpu.get_barrier_semaphore()
    for d in range(1, W):
        pl.semaphore_signal(barrier, inc=1, device_id=(lax.rem(me + d, W), ml), device_id_type=MESH)
    for d in range(1, NL):
        pl.semaphore_signal(barrier, inc=1, device_id=(me, lax.rem(ml + d, NL)), device_id_type=MESH)
    pl.semaphore_wait(barrier, W - 1 + NL - 1)

    def in_copy(s, d):
        dst = lax.rem(me + d, W)
        return pltpu.make_async_remote_copy(
            src_ref=packed_ref.at[dst * SL + s], dst_ref=recv.at[s, me],
            send_sem=in_send.at[s, d], recv_sem=in_recv.at[s, d],
            device_id=(dst, ml), device_id_type=MESH)

    def in_arrival(s, d):
        src = lax.rem(me + W - d, W)
        return pltpu.make_async_remote_copy(
            src_ref=packed_ref.at[me * SL + s], dst_ref=recv.at[s, src],
            send_sem=in_send.at[s, d], recv_sem=in_recv.at[s, d],
            device_id=(src, ml), device_id_type=MESH)

    def out_copy(s, d):
        dst = lax.rem(me + d, W)
        return pltpu.make_async_remote_copy(
            src_ref=osend.at[s, dst], dst_ref=out_ref.at[me * SL + s],
            send_sem=out_send.at[s, d], recv_sem=out_recv.at[s, d],
            device_id=(dst, ml), device_id_type=MESH)

    def out_arrival(s, d):
        src = lax.rem(me + W - d, W)
        return pltpu.make_async_remote_copy(
            src_ref=osend.at[s, src], dst_ref=out_ref.at[src * SL + s],
            send_sem=out_send.at[s, d], recv_sem=out_recv.at[s, d],
            device_id=(src, ml), device_id_type=MESH)

    def lev_copy(s, d):
        dst = lax.rem(ml + d, NL)
        return pltpu.make_async_remote_copy(
            src_ref=lev_send.at[s, dst], dst_ref=lev_recv.at[s, ml],
            send_sem=lev_ssem.at[s, d], recv_sem=lev_rsem.at[s, d],
            device_id=(me, dst), device_id_type=MESH)

    def lev_arrival(s, d):
        src = lax.rem(ml + NL - d, NL)
        return pltpu.make_async_remote_copy(
            src_ref=lev_send.at[s, src], dst_ref=lev_recv.at[s, src],
            send_sem=lev_ssem.at[s, d], recv_sem=lev_rsem.at[s, d],
            device_id=(me, src), device_id_type=MESH)

    def own_in(s):
        return pltpu.make_async_copy(packed_ref.at[me * SL + s], recv.at[s, me], own_sem.at[s])

    def own_out(s):
        return pltpu.make_async_copy(osend.at[s, me], out_ref.at[me * SL + s], out_own.at[s])

    def table_in(s):
        return pltpu.make_async_copy(tables_ref.at[s], tab.at[s], tab_sem.at[s])

    @pl.loop(0, SL)
    def _(s):
        for d in order:
            in_copy(s, d).start()
        own_in(s).start()
        table_in(s).start()

    rows = PAIR * LP * NL
    levels = LP * NL
    up = (iota((rows, levels), 0) // PAIR == iota((rows, levels), 1)).astype(jnp.float32)
    down = (iota((LP, C), 0) == iota((LP, C), 1) // FIELDS).astype(jnp.float32)
    wide = jnp.dot(
        jnp.dot(up, coupling_ref[...], precision=lax.Precision.HIGHEST), down,
        precision=lax.Precision.HIGHEST)
    kept = iota((rows, C), 1) % FIELDS == iota((rows, C), 0) % PAIR + FIRST
    k_high[...], k_low[...] = split(jnp.where(kept, wide, 0.0))
    er, ec = iota((C, rows), 0), iota((C, rows), 1) % (PAIR * LP)
    expand = ((er // FIELDS == ec // PAIR) & (er % FIELDS == ec % PAIR + FIRST)).astype(jnp.float32)
    expand = expand.astype(jnp.bfloat16)
    flip = (iota((TW, TW), 0) + iota((TW, TW), 1) == TW - 1).astype(jnp.float32).astype(jnp.bfloat16)

    def flipped(v):
        high, low = split(v)
        return mm(high, flip) + mm(low, flip)

    @pl.loop(0, SL)
    def _(s):
        wave = wave_ref[me * SL + s]
        first = tile_ref[s] * TILE
        m = (wave * N) // waves
        for d in order:
            in_arrival(s, d).wait_recv()
        own_in(s).wait()
        table_in(s).wait()

        for t in range(nt):
            north = jnp.concatenate([recv[s, t * BPT + b] for b in range(BPT)], axis=1)
            south = jnp.concatenate([recv[s, half + t * BPT + b] for b in range(BPT)], axis=1)
            south = flipped(south)
            for v, at, row in ((north, t, 0), (south, nt - 1 - t, C)):
                lanes = pl.ds(at * TW, TW)
                used = iota((1, TW), 1) + at * TW >= first
                scaled = v * jnp.where(used, gauss_ref[:, lanes], 0.0)
                high, low = split(scaled)
                x_high[pl.ds(row, C), lanes] = high
                x_low[pl.ds(row, C), lanes] = low

        @pl.loop(0, N // NW)
        def _(j):
            lanes = pl.ds(pl.multiple_of(j * NW, NW), NW)
            t_high, t_low = split(tab[s, :, lanes])
            f = mm3(x_high[...], x_low[...], t_high, t_low)
            degree = iota((1, NW), 1) + j * NW
            used = degree >= m
            sign = jnp.where((degree + m) % 2 == 0, 1.0, -1.0)
            spectral = jnp.where(used, f[:C] + sign * f[C:], 0.0)
            spec[:, lanes] = spectral
            s_high, s_low = split(spectral)
            part = mm3(k_high[...], k_low[...], s_high, s_low)
            for l in range(NL):
                lev_send[s, l, :, lanes] = part[l * PAIR * LP:(l + 1) * PAIR * LP]

        lev_recv[s, ml] = lev_send[s, ml]
        for d in lev_order:
            lev_copy(s, d).start()
        for d in lev_order:
            lev_arrival(s, d).wait_recv()

        @pl.loop(0, N // NW)
        def _(j):
            lanes = pl.ds(pl.multiple_of(j * NW, NW), NW)
            degree = iota((1, NW), 1) + j * NW
            sign = jnp.where((degree + m) % 2 == 0, 1.0, -1.0)
            factor = (degree * (degree + 1)).astype(jnp.float32) / float(N * (N - 1))
            p_high, p_low = split(jnp.concatenate([lev_recv[s, l, :, lanes] for l in range(NL)], axis=0))
            coupled = mm(expand, p_high) + mm(expand, p_low)
            updated = spec[:, lanes] - factor * coupled
            u_high, u_low = split(updated)
            r_high[pl.ds(0, C), lanes] = u_high
            r_low[pl.ds(0, C), lanes] = u_low
            w_high, w_low = split(sign * updated)
            r_high[pl.ds(C, C), lanes] = w_high
            r_low[pl.ds(C, C), lanes] = w_low

        @pl.loop(0, nt)
        def _(i):
            rows_here = pl.ds(pl.multiple_of(i * TW, TW), TW)
            t_high, t_low = split(tab[s, rows_here, :])
            o = mm3(r_high[...], r_low[...], t_high, t_low, NT)
            used = iota((1, TW), 1) + i * TW >= first
            o = jnp.where(used, o, 0.0)
            north = o[:C]
            south = flipped(o[C:])
            for b in range(BPT):
                cut = slice(b * LAT, (b + 1) * LAT)
                osend[s, i * BPT + b] = north[:, cut]
                osend[s, half + (nt - 1 - i) * BPT + b] = south[:, cut]

        for d in order:
            out_copy(s, d).start()
        own_out(s).start()

    @pl.loop(0, SL)
    def _(s):
        own_out(s).wait()
        for d in order:
            in_copy(s, d).wait_send()
            out_copy(s, d).wait_send()
            out_arrival(s, d).wait_recv()
        for d in lev_order:
            lev_copy(s, d).wait_send()


def transform(W, NL, packed, legendre, gauss_weights, wave_of_slot, first_tile, coupling):
    waves, C, LAT = packed.shape
    SL, H, N = legendre.shape
    rows = PAIR * (C // FIELDS)
    f32, bf16, dma = jnp.float32, jnp.bfloat16, pltpu.SemaphoreType.DMA
    vmem = pl.BlockSpec(memory_space=pltpu.VMEM)
    smem = pl.BlockSpec(memory_space=pltpu.SMEM)
    hbm = pl.BlockSpec(memory_space=pl.ANY)
    return pl.pallas_call(
        functools.partial(spectral_kernel, W, NL),
        out_shape=jax.ShapeDtypeStruct((waves, C, LAT), f32),
        in_specs=[smem, smem, vmem, vmem, hbm, hbm],
        out_specs=hbm,
        scratch_shapes=[
            pltpu.VMEM((SL, H, N), f32),
            pltpu.VMEM((SL, W, C, LAT), f32),
            pltpu.VMEM((SL, W, C, LAT), f32),
            pltpu.VMEM((SL, NL, rows, N), f32),
            pltpu.VMEM((SL, NL, rows, N), f32),
            pltpu.VMEM((2 * C, H), bf16),
            pltpu.VMEM((2 * C, H), bf16),
            pltpu.VMEM((C, N), f32),
            pltpu.VMEM((2 * C, N), bf16),
            pltpu.VMEM((2 * C, N), bf16),
            pltpu.VMEM((rows * NL, C), bf16),
            pltpu.VMEM((rows * NL, C), bf16),
            dma((SL,)), dma((SL,)),
            dma((SL, W)), dma((SL, W)),
            dma((SL, NL)), dma((SL, NL)),
            dma((SL,)), dma((SL, W)), dma((SL, W)),
        ],
        compiler_params=pltpu.CompilerParams(
            collective_id=0, has_side_effects=True, vmem_limit_bytes=VMEM_BYTES),
        name="spectral",
    )(wave_of_slot, first_tile, gauss_weights[None, :], coupling, packed, legendre)


def solution(mesh):
    W, NL = mesh.shape["wave"], mesh.shape["lev"]

    def shards(grid_data, legendre, gauss_weights, wave_of_slot, first_tile, coupling):
        packed = pack(wave_of_slot, grid_data)
        back = transform(W, NL, packed, legendre, gauss_weights, wave_of_slot, first_tile, coupling)
        return unpack(wave_of_slot, back)

    placed = (P("wave", None, "lev"), P("wave", None, None), P(), P(), P("wave"), P(None, "lev"))
    return jax.shard_map(
        shards, mesh=mesh, in_specs=placed, out_specs=P("wave", None, "lev"), check_vma=False
    )
```

profile of v0, /device:TPU:0, one launch (start us, length us, event | category | flops | bytes accessed | tf_op | source)
XLA Modules:
  0.0 189.5 jit_solution(6342250223110785164)
XLA Ops:
  0.0 5.2 %copy.7 = f32[256,32,96]{2,1,0:T(8,128)} copy(f32[256,32,96]{0,2,1:T(8,128)} %param.6) | data formatting | bytes 6291456 | tf_op args[0]
  5.2 0.0 copy-start
  5.2 16.6 %pack.1.packed_ref = f32[32,96,256]{2,1,0:T(8,128)} custom-call(s32[32]{0:T(128)} %wave_ref.5, f32[8192,96]{1,0:T(8,128)} %bitcast.4), custom_call_target="tpu_custom_call" | custom-call | tf_op jit(solution)/shard_map/pack/pallas_call | solution.py:46
  21.8 0.0 copy-done
  21.8 0.7 copy.8.coupling_ref
  22.5 141.5 %spectral.1.y_ref = f32[32,96,256]{2,1,0:T(8,128)} custom-call(s32[32]{0:T(128)} %wave_ref.5, s32[4]{0:T(128)} %tile_ref.1, f32[1,1024]{1,0:T(1,128)} %bitcast.5, f32[64,16]{1,0:T(8,128)} %copy.8.coupling_ref, f32[32,96,256]{2,1,0:T(8,128)} %pack.1.packed_ref, f32[4,1024,1024]{2,1,0:T(8,128)} %tables_ref.1), custom_call_target="tpu_custom_call" | custom-call | tf_op jit(solution)/shard_map/spectral/pallas_call | solution.py:283
  164.0 20.5 %unpack.1 = f32[8192,96]{1,0:T(8,128)} custom-call(s32[32]{0:T(128)} %wave_ref.5, f32[32,96,256]{2,1,0:T(8,128)} %spectral.1.y_ref), custom_call_target="tpu_custom_call" | custom-call | tf_op jit(solution)/shard_map/unpack/pallas_call | solution.py:69
  184.5 5.0 %copy.9 = f32[256,32,96]{0,2,1:T(8,128)} copy(f32[256,32,96]{2,1,0:T(8,128)} %bitcast.3) | data formatting | bytes 6291456 | tf_op jit(solution)/shard_map/reshape | solution.py:81
Async XLA Ops:
  5.2 16.6 %copy-start = (f32[64,16]{0,1:T(8,128)S(1)}, f32[64,16]{0,1:T(8,128)}, u32[]{:S(2)}) copy-start(f32[64,16]{0,1:T(8,128)} %param.11) | copy-start | bytes 12292
where the time goes:
time: 191 us; the launch traced here: 189 us
  Pallas kernels  179 us (94%)
  local copies, waits for them, and re-layouts  10.9 us (6%)
    pallas_call x1, Pallas kernels, transform(): pl.pallas_call(functools.partial(spectral_kernel, W, NL), out_shape=jax.S...  142 us
    pallas_call x1, Pallas kernels, unpack(): pl.pallas_call(unpack_kernel, grid_spec=pltpu.PrefetchScalarGridSpec(num_...  20.5 us
    pallas_call x1, Pallas kernels, pack(): pl.pallas_call(pack_kernel, grid_spec=pltpu.PrefetchScalarGridSpec(num_sc...  16.6 us
    unnamed x4, local copies, waits for them, and re-layouts  5.93 us
    reshape x1, local copies, waits for them, and re-layouts, unpack(): return out.reshape(lats, waves, cols)  4.96 us

commit v1 on v0

--- a/solution.py
+++ b/solution.py
@@ -34,58 +34,51 @@
     return lax.broadcasted_iota(jnp.int32, shape, axis)
 
 
-def pack_kernel(wave_ref, x_ref, out_ref):
+def unpack_kernel(wave_ref, y_ref, out_ref, held, in_sem, out_sem):
     waves = wave_ref.shape[0]
-    lats = out_ref.shape[2]
-    wave = wave_ref[pl.program_id(0)]
-    out_ref[0] = x_ref[pl.ds(wave, lats, stride=waves), :].T
-
-
-def pack(wave_of_slot, grid_data):
-    lats, waves, cols = grid_data.shape
+
+    def fetch(s):
+        return pltpu.make_async_copy(y_ref.at[s], held.at[s], in_sem.at[s])
+
+    def put(s):
+        return pltpu.make_async_copy(held.at[s], out_ref.at[wave_ref[s]], out_sem.at[s])
+
+    @pl.loop(0, waves)
+    def _(s):
+        fetch(s).start()
+
+    @pl.loop(0, waves)
+    def _(s):
+        fetch(s).wait()
+        put(s).start()
+
+    @pl.loop(0, waves)
+    def _(s):
+        put(s).wait()
+
+
+def unpack(wave_of_slot, packed):
+    waves = packed.shape[0]
     return pl.pallas_call(
-        pack_kernel,
-        grid_spec=pltpu.PrefetchScalarGridSpec(
-            num_scalar_prefetch=1,
-            grid=(waves,),
-            in_specs=[pl.BlockSpec((lats * waves, cols), lambda s, w: (0, 0))],
-            out_specs=pl.BlockSpec((1, cols, lats), lambda s, w: (s, 0, 0)),
-        ),
-        out_shape=jax.ShapeDtypeStruct((waves, cols, lats), jnp.float32),
-        compiler_params=pltpu.CompilerParams(vmem_limit_bytes=VMEM_BYTES),
-        name="pack",
-    )(wave_of_slot, grid_data.reshape(lats * waves, cols))
-
-
-def unpack_kernel(wave_ref, y_ref, out_ref):
-    waves = wave_ref.shape[0]
-    lats = y_ref.shape[2]
-    wave = wave_ref[pl.program_id(0)]
-    out_ref[pl.ds(wave, lats, stride=waves), :] = y_ref[0].T
-
-
-def unpack(wave_of_slot, packed):
-    waves, cols, lats = packed.shape
-    out = pl.pallas_call(
         unpack_kernel,
-        grid_spec=pltpu.PrefetchScalarGridSpec(
-            num_scalar_prefetch=1,
-            grid=(waves,),
-            in_specs=[pl.BlockSpec((1, cols, lats), lambda s, w: (s, 0, 0))],
-            out_specs=pl.BlockSpec((lats * waves, cols), lambda s, w: (0, 0)),
-        ),
-        out_shape=jax.ShapeDtypeStruct((lats * waves, cols), jnp.float32),
+        out_shape=jax.ShapeDtypeStruct(packed.shape, jnp.float32),
+        in_specs=[pl.BlockSpec(memory_space=pltpu.SMEM), pl.BlockSpec(memory_space=pl.ANY)],
+        out_specs=pl.BlockSpec(memory_space=pl.ANY),
+        scratch_shapes=[
+            pltpu.VMEM(packed.shape, jnp.float32),
+            pltpu.SemaphoreType.DMA((waves,)),
+            pltpu.SemaphoreType.DMA((waves,)),
+        ],
         compiler_params=pltpu.CompilerParams(vmem_limit_bytes=VMEM_BYTES),
         name="unpack",
     )(wave_of_slot, packed)
-    return out.reshape(lats, waves, cols)
 
 
 def spectral_kernel(
     W, NL,
-    wave_ref, tile_ref, gauss_ref, coupling_ref, packed_ref, tables_ref, out_ref,
-    tab, recv, osend, lev_send, lev_recv, x_high, x_low, spec, r_high, r_low, k_high, k_low,
-    tab_sem, own_sem, in_send, in_recv, lev_ssem, lev_rsem, out_own, out_send, out_recv,
+    wave_ref, tile_ref, gauss_ref, coupling_ref, grid_ref, tables_ref, out_ref,
+    held, stage, tab, recv, osend, lev_send, lev_recv, x_high, x_low, spec, r_high, r_low, k_high, k_low,
+    held_sem, tab_sem, own_sem, in_send, in_recv, lev_ssem, lev_rsem, out_own, out_send, out_recv,
 ):
     SL, H, N = tab.shape
     C, LAT = recv.shape[2], recv.shape[3]
@@ -101,6 +94,8 @@
     order = sorted(range(1, W), key=lambda d: (abs(d - half), d))
     lev_order = sorted(range(1, NL), key=lambda d: (abs(d - NL // 2), d))
 
+    held_copy = pltpu.make_async_copy(grid_ref, held, held_sem)
+    held_copy.start()
     barrier = pltpu.get_barrier_semaphore()
     for d in range(1, W):
         pl.semaphore_signal(barrier, inc=1, device_id=(lax.rem(me + d, W), ml), device_id_type=MESH)
@@ -111,14 +106,14 @@
     def in_copy(s, d):
         dst = lax.rem(me + d, W)
         return pltpu.make_async_remote_copy(
-            src_ref=packed_ref.at[dst * SL + s], dst_ref=recv.at[s, me],
+            src_ref=stage.at[dst * SL + s], dst_ref=recv.at[s, me],
             send_sem=in_send.at[s, d], recv_sem=in_recv.at[s, d],
             device_id=(dst, ml), device_id_type=MESH)
 
     def in_arrival(s, d):
         src = lax.rem(me + W - d, W)
         return pltpu.make_async_remote_copy(
-            src_ref=packed_ref.at[me * SL + s], dst_ref=recv.at[s, src],
+            src_ref=stage.at[me * SL + s], dst_ref=recv.at[s, src],
             send_sem=in_send.at[s, d], recv_sem=in_recv.at[s, d],
             device_id=(src, ml), device_id_type=MESH)
 
@@ -151,13 +146,19 @@
             device_id=(me, src), device_id_type=MESH)
 
     def own_in(s):
-        return pltpu.make_async_copy(packed_ref.at[me * SL + s], recv.at[s, me], own_sem.at[s])
+        return pltpu.make_async_copy(stage.at[me * SL + s], recv.at[s, me], own_sem.at[s])
 
     def own_out(s):
         return pltpu.make_async_copy(osend.at[s, me], out_ref.at[me * SL + s], out_own.at[s])
 
     def table_in(s):
         return pltpu.make_async_copy(tables_ref.at[s], tab.at[s], tab_sem.at[s])
+
+    held_copy.wait()
+
+    @pl.loop(0, waves)
+    def _(s):
+        stage[s] = held[wave_ref[s]]
 
     @pl.loop(0, SL)
     def _(s):
@@ -171,7 +172,7 @@
     up = (iota((rows, levels), 0) // PAIR == iota((rows, levels), 1)).astype(jnp.float32)
     down = (iota((LP, C), 0) == iota((LP, C), 1) // FIELDS).astype(jnp.float32)
     wide = jnp.dot(
-        jnp.dot(up, coupling_ref[...], precision=lax.Precision.HIGHEST), down,
+        lax.dot_general(up, coupling_ref[...], NT, precision=lax.Precision.HIGHEST), down,
         precision=lax.Precision.HIGHEST)
     kept = iota((rows, C), 1) % FIELDS == iota((rows, C), 0) % PAIR + FIRST
     k_high[...], k_low[...] = split(jnp.where(kept, wide, 0.0))
@@ -272,8 +273,8 @@
             lev_copy(s, d).wait_send()
 
 
-def transform(W, NL, packed, legendre, gauss_weights, wave_of_slot, first_tile, coupling):
-    waves, C, LAT = packed.shape
+def transform(W, NL, grid, legendre, gauss_weights, wave_of_slot, first_tile, coupling):
+    waves, C, LAT = grid.shape
     SL, H, N = legendre.shape
     rows = PAIR * (C // FIELDS)
     f32, bf16, dma = jnp.float32, jnp.bfloat16, pltpu.SemaphoreType.DMA
@@ -286,6 +287,8 @@
         in_specs=[smem, smem, vmem, vmem, hbm, hbm],
         out_specs=hbm,
         scratch_shapes=[
+            pltpu.VMEM((waves, C, LAT), f32),
+            pltpu.VMEM((waves, C, LAT), f32),
             pltpu.VMEM((SL, H, N), f32),
             pltpu.VMEM((SL, W, C, LAT), f32),
             pltpu.VMEM((SL, W, C, LAT), f32),
@@ -298,7 +301,7 @@
             pltpu.VMEM((2 * C, N), bf16),
             pltpu.VMEM((rows * NL, C), bf16),
             pltpu.VMEM((rows * NL, C), bf16),
-            dma((SL,)), dma((SL,)),
+            dma, dma((SL,)), dma((SL,)),
             dma((SL, W)), dma((SL, W)),
             dma((SL, NL)), dma((SL, NL)),
             dma((SL,)), dma((SL, W)), dma((SL, W)),
@@ -306,16 +309,16 @@
         compiler_params=pltpu.CompilerParams(
             collective_id=0, has_side_effects=True, vmem_limit_bytes=VMEM_BYTES),
         name="spectral",
-    )(wave_of_slot, first_tile, gauss_weights[None, :], coupling, packed, legendre)
+    )(wave_of_slot, first_tile, gauss_weights[None, :], coupling.T, grid, legendre)
 
 
 def solution(mesh):
     W, NL = mesh.shape["wave"], mesh.shape["lev"]
 
     def shards(grid_data, legendre, gauss_weights, wave_of_slot, first_tile, coupling):
-        packed = pack(wave_of_slot, grid_data)
-        back = transform(W, NL, packed, legendre, gauss_weights, wave_of_slot, first_tile, coupling)
-        return unpack(wave_of_slot, back)
+        grid = jnp.transpose(grid_data, (1, 2, 0))
+        back = transform(W, NL, grid, legendre, gauss_weights, wave_of_slot, first_tile, coupling)
+        return jnp.transpose(unpack(wave_of_slot, back), (2, 0, 1))
 
     placed = (P("wave", None, "lev"), P("wave", None, None), P(), P(), P("wave"), P(None, "lev"))
     return jax.shard_map(

time: 191 us -> 147 us (0.77)
  Pallas kernels: 179 us -> 146 us
  local copies, waits for them, and re-layouts: 10.9 us -> 0 us
    pallas_call x2 -> x1, Pallas kernels: 37 us -> 4.19 us  [unpack(): pl.pallas_call(unpack_kernel, out_shape=jax.ShapeDtypeStruct(packed.shape...]
    unnamed x4 -> x0, local copies, waits for them, and re-layouts: 5.93 us -> none
    reshape x1 -> x0, local copies, waits for them, and re-layouts: 4.96 us -> none  [unpack(): return out.reshape(lats, waves, cols)]
where the time goes in v1:
time: 147 us; the launch traced here: 146 us
  Pallas kernels  146 us (99%)
    pallas_call x1, Pallas kernels, transform(): pl.pallas_call(functools.partial(spectral_kernel, W, NL), out_shape=jax.S...  142 us
    pallas_call x1, Pallas kernels, unpack(): pl.pallas_call(unpack_kernel, out_shape=jax.ShapeDtypeStruct(packed.shape...  4.19 us

profile of v1, /device:TPU:0, one launch (start us, length us, event | category | flops | bytes accessed | tf_op | source)
XLA Modules:
  0.0 146.2 jit_solution(12402217400629246525)
XLA Ops:
  0.0 142.0 %spectral.1.y_ref = f32[32,96,256]{2,1,0:T(8,128)} custom-call(s32[32]{0:T(128)} %wave_ref.3, s32[4]{0:T(128)} %tile_ref.1, f32[1,1024]{1,0:T(1,128)} %bitcast.6, f32[16,64]{1,0:T(8,128)} %bitcast.5, f32[32,96,256]{2,1,0:T(8,128)} %bitcast.4, f32[4,1024,1024]{2,1,0:T(8,128)} %tables_ref.1), custom_call_target="tpu_custom_call" | custom-call | tf_op jit(solution)/shard_map/spectral/pallas_call | solution.py:284
  142.0 4.2 %unpack.1 = f32[32,96,256]{2,1,0:T(8,128)} custom-call(s32[32]{0:T(128)} %wave_ref.3, f32[32,96,256]{2,1,0:T(8,128)} %spectral.1.y_ref), custom_call_target="tpu_custom_call" | custom-call | tf_op jit(solution)/shard_map/unpack/pallas_call | solution.py:62

commit v2 on v1

--- a/solution.py
+++ b/solution.py
@@ -34,51 +34,75 @@
     return lax.broadcasted_iota(jnp.int32, shape, axis)
 
 
-def unpack_kernel(wave_ref, y_ref, out_ref, held, in_sem, out_sem):
+def polar(w, W):
+    return (w < W // 4) | (w >= W - W // 4)
+
+
+def unpack_kernel(W, compact, wave_ref, y_ref, out_ref, held, zero, in_sem, out_sem):
     waves = wave_ref.shape[0]
+    halved = polar(lax.axis_index("wave"), W) if compact else False
+
+    def source(s):
+        return jnp.where(halved, s - s % 2, s) if compact else s
 
     def fetch(s):
-        return pltpu.make_async_copy(y_ref.at[s], held.at[s], in_sem.at[s])
-
-    def put(s):
-        return pltpu.make_async_copy(held.at[s], out_ref.at[wave_ref[s]], out_sem.at[s])
+        return pltpu.make_async_copy(y_ref.at[source(s)], held.at[s], in_sem.at[s])
+
+    def put(s, src):
+        return pltpu.make_async_copy(src, out_ref.at[wave_ref[s]], out_sem.at[s])
 
     @pl.loop(0, waves)
     def _(s):
         fetch(s).start()
 
+    if compact:
+        zero[...] = jnp.zeros_like(zero)
+
     @pl.loop(0, waves)
     def _(s):
         fetch(s).wait()
-        put(s).start()
+        if compact:
+            empty = halved & (wave_ref[s] > wave_ref[s + 1 - 2 * (s % 2)])
+
+            @pl.when(empty)
+            def _():
+                put(s, zero).start()
+
+            @pl.when(jnp.logical_not(empty))
+            def _():
+                put(s, held.at[s]).start()
+        else:
+            put(s, held.at[s]).start()
 
     @pl.loop(0, waves)
     def _(s):
-        put(s).wait()
-
-
-def unpack(wave_of_slot, packed):
+        put(s, held.at[s]).wait()
+
+
+def unpack(W, compact, wave_of_slot, packed):
     waves = packed.shape[0]
     return pl.pallas_call(
-        unpack_kernel,
+        functools.partial(unpack_kernel, W, compact),
         out_shape=jax.ShapeDtypeStruct(packed.shape, jnp.float32),
         in_specs=[pl.BlockSpec(memory_space=pltpu.SMEM), pl.BlockSpec(memory_space=pl.ANY)],
         out_specs=pl.BlockSpec(memory_space=pl.ANY),
         scratch_shapes=[
             pltpu.VMEM(packed.shape, jnp.float32),
+            pltpu.VMEM(packed.shape[1:], jnp.float32),
             pltpu.SemaphoreType.DMA((waves,)),
             pltpu.SemaphoreType.DMA((waves,)),
         ],
         compiler_params=pltpu.CompilerParams(vmem_limit_bytes=VMEM_BYTES),
-        name="unpack",
+        name="unpack_half" if compact else "unpack",
     )(wave_of_slot, packed)
 
 
 def spectral_kernel(
-    W, NL,
-    wave_ref, tile_ref, gauss_ref, coupling_ref, grid_ref, tables_ref, out_ref,
+    W, NL, compact,
+    wave_ref, tile_ref, gauss_ref, coupling_ref, grid_ref, tables_ref, out_ref, flag_ref,
     held, stage, tab, recv, osend, lev_send, lev_recv, x_high, x_low, spec, r_high, r_low, k_high, k_low,
     held_sem, tab_sem, own_sem, in_send, in_recv, lev_ssem, lev_rsem, out_own, out_send, out_recv,
+    flags, flag_send, flag_recv,
 ):
     SL, H, N = tab.shape
     C, LAT = recv.shape[2], recv.shape[3]
@@ -96,6 +120,15 @@
 
     held_copy = pltpu.make_async_copy(grid_ref, held, held_sem)
     held_copy.start()
+    def halved(w):
+        return polar(w, W) if compact else False
+
+    def full_turn(w, s, parity):
+        return jnp.logical_not(halved(w)) | (s % 2 == parity) if compact else s >= 0
+
+    def block(w, s):
+        return jnp.where(halved(w), s - s % 2, s) if compact else s
+
     barrier = pltpu.get_barrier_semaphore()
     for d in range(1, W):
         pl.semaphore_signal(barrier, inc=1, device_id=(lax.rem(me + d, W), ml), device_id_type=MESH)
@@ -120,14 +153,14 @@
     def out_copy(s, d):
         dst = lax.rem(me + d, W)
         return pltpu.make_async_remote_copy(
-            src_ref=osend.at[s, dst], dst_ref=out_ref.at[me * SL + s],
+            src_ref=osend.at[block(dst, s), dst], dst_ref=out_ref.at[me * SL + block(dst, s)],
             send_sem=out_send.at[s, d], recv_sem=out_recv.at[s, d],
             device_id=(dst, ml), device_id_type=MESH)
 
     def out_arrival(s, d):
         src = lax.rem(me + W - d, W)
         return pltpu.make_async_remote_copy(
-            src_ref=osend.at[s, src], dst_ref=out_ref.at[src * SL + s],
+            src_ref=osend.at[block(me, s), src], dst_ref=out_ref.at[src * SL + block(me, s)],
             send_sem=out_send.at[s, d], recv_sem=out_recv.at[s, d],
             device_id=(src, ml), device_id_type=MESH)
 
@@ -149,23 +182,56 @@
         return pltpu.make_async_copy(stage.at[me * SL + s], recv.at[s, me], own_sem.at[s])
 
     def own_out(s):
-        return pltpu.make_async_copy(osend.at[s, me], out_ref.at[me * SL + s], out_own.at[s])
+        return pltpu.make_async_copy(
+            osend.at[block(me, s), me], out_ref.at[me * SL + block(me, s)], out_own.at[s])
+
+    def flag_copy(d):
+        dst = lax.rem(me + d, W)
+        return pltpu.make_async_remote_copy(
+            src_ref=flags.at[W], dst_ref=flags.at[me], send_sem=flag_send.at[d], recv_sem=flag_recv.at[d],
+            device_id=(dst, ml), device_id_type=MESH)
+
+    def flag_arrival(d):
+        src = lax.rem(me + W - d, W)
+        return pltpu.make_async_remote_copy(
+            src_ref=flags.at[W], dst_ref=flags.at[src], send_sem=flag_send.at[d], recv_sem=flag_recv.at[d],
+            device_id=(src, ml), device_id_type=MESH)
 
     def table_in(s):
         return pltpu.make_async_copy(tables_ref.at[s], tab.at[s], tab_sem.at[s])
 
+    if compact:
+        held_enough = jnp.float32(1)
+        for s in range(0, SL, 2):
+            even, odd = wave_ref[me * SL + s], wave_ref[me * SL + s + 1]
+            late = jnp.where(even > odd, tile_ref[s], tile_ref[s + 1])
+            held_enough = jnp.where(late * TILE >= H // 2, held_enough, jnp.float32(0))
+        flags[W] = jnp.full(flags.shape[1:], held_enough)
+        flags[me] = jnp.full(flags.shape[1:], held_enough)
+
     held_copy.wait()
 
     @pl.loop(0, waves)
     def _(s):
-        stage[s] = held[wave_ref[s]]
+        wave = wave_ref[s]
+        if compact:
+            partner = wave_ref[s + 1 - 2 * (s % 2)]
+            wave = jnp.where(halved(me), jnp.minimum(wave, partner), wave)
+        stage[s] = held[wave]
 
     @pl.loop(0, SL)
     def _(s):
-        for d in order:
-            in_copy(s, d).start()
+        @pl.when(full_turn(me, s, 0))
+        def _():
+            for d in order:
+                in_copy(s, d).start()
+
         own_in(s).start()
         table_in(s).start()
+
+    if compact:
+        for d in order:
+            flag_copy(d).start()
 
     rows = PAIR * LP * NL
     levels = LP * NL
@@ -191,13 +257,18 @@
         first = tile_ref[s] * TILE
         m = (wave * N) // waves
         for d in order:
-            in_arrival(s, d).wait_recv()
+            @pl.when(full_turn(lax.rem(me + W - d, W), s, 0))
+            def _():
+                in_arrival(s, d).wait_recv()
+
         own_in(s).wait()
         table_in(s).wait()
 
         for t in range(nt):
-            north = jnp.concatenate([recv[s, t * BPT + b] for b in range(BPT)], axis=1)
-            south = jnp.concatenate([recv[s, half + t * BPT + b] for b in range(BPT)], axis=1)
+            w_north = [t * BPT + b for b in range(BPT)]
+            w_south = [half + w for w in w_north]
+            north = jnp.concatenate([recv[s - s % 2 if halved(w) else s, w] for w in w_north], axis=1)
+            south = jnp.concatenate([recv[s - s % 2 if halved(w) else s, w] for w in w_south], axis=1)
             south = flipped(south)
             for v, at, row in ((north, t, 0), (south, nt - 1 - t, C)):
                 lanes = pl.ds(at * TW, TW)
@@ -253,27 +324,66 @@
             o = jnp.where(used, o, 0.0)
             north = o[:C]
             south = flipped(o[C:])
-            for b in range(BPT):
-                cut = slice(b * LAT, (b + 1) * LAT)
-                osend[s, i * BPT + b] = north[:, cut]
-                osend[s, half + (nt - 1 - i) * BPT + b] = south[:, cut]
+
+            def store(at, add):
+                for b in range(BPT):
+                    cut = slice(b * LAT, (b + 1) * LAT)
+                    for w, v in ((i * BPT + b, north), (half + (nt - 1 - i) * BPT + b, south)):
+                        osend[at, w] = osend[at, w] + v[:, cut] if add else v[:, cut]
+
+            if compact:
+                second = (i < nt // 2) & (s % 2 == 1)
+
+                @pl.when(second)
+                def _():
+                    store(s - 1, True)
+
+                @pl.when(jnp.logical_not(second))
+                def _():
+                    store(s, False)
+            else:
+                store(s, False)
 
         for d in order:
-            out_copy(s, d).start()
-        own_out(s).start()
+            @pl.when(full_turn(lax.rem(me + d, W), s, 1))
+            def _():
+                out_copy(s, d).start()
+
+        @pl.when(full_turn(me, s, 1))
+        def _():
+            own_out(s).start()
 
     @pl.loop(0, SL)
     def _(s):
-        own_out(s).wait()
+        @pl.when(full_turn(me, s, 0))
+        def _():
+            for d in order:
+                in_copy(s, d).wait_send()
+
+        @pl.when(full_turn(me, s, 1))
+        def _():
+            own_out(s).wait()
+            for d in order:
+                out_arrival(s, d).wait_recv()
+
         for d in order:
-            in_copy(s, d).wait_send()
-            out_copy(s, d).wait_send()
-            out_arrival(s, d).wait_recv()
+            @pl.when(full_turn(lax.rem(me + d, W), s, 1))
+            def _():
+                out_copy(s, d).wait_send()
+
         for d in lev_order:
             lev_copy(s, d).wait_send()
 
-
-def transform(W, NL, grid, legendre, gauss_weights, wave_of_slot, first_tile, coupling):
+    if compact:
+        for d in order:
+            flag_copy(d).wait_send()
+            flag_arrival(d).wait_recv()
+        flag_ref[...] = functools.reduce(jnp.minimum, [flags[w] for w in range(W)])
+    else:
+        flag_ref[...] = jnp.ones_like(flag_ref)
+
+
+def transform(W, NL, compact, grid, legendre, gauss_weights, wave_of_slot, first_tile, coupling):
     waves, C, LAT = grid.shape
     SL, H, N = legendre.shape
     rows = PAIR * (C // FIELDS)
@@ -282,10 +392,11 @@
     smem = pl.BlockSpec(memory_space=pltpu.SMEM)
     hbm = pl.BlockSpec(memory_space=pl.ANY)
     return pl.pallas_call(
-        functools.partial(spectral_kernel, W, NL),
-        out_shape=jax.ShapeDtypeStruct((waves, C, LAT), f32),
+        functools.partial(spectral_kernel, W, NL, compact),
+        out_shape=(
+            jax.ShapeDtypeStruct((waves, C, LAT), f32), jax.ShapeDtypeStruct((8, 128), f32)),
         in_specs=[smem, smem, vmem, vmem, hbm, hbm],
-        out_specs=hbm,
+        out_specs=(hbm, vmem),
         scratch_shapes=[
             pltpu.VMEM((waves, C, LAT), f32),
             pltpu.VMEM((waves, C, LAT), f32),
@@ -305,10 +416,11 @@
             dma((SL, W)), dma((SL, W)),
             dma((SL, NL)), dma((SL, NL)),
             dma((SL,)), dma((SL, W)), dma((SL, W)),
+            pltpu.VMEM((W + 1, 8, 128), f32), dma((W,)), dma((W,)),
         ],
         compiler_params=pltpu.CompilerParams(
-            collective_id=0, has_side_effects=True, vmem_limit_bytes=VMEM_BYTES),
-        name="spectral",
+            collective_id=0 if compact else 1, has_side_effects=True, vmem_limit_bytes=VMEM_BYTES),
+        name="spectral_half" if compact else "spectral",
     )(wave_of_slot, first_tile, gauss_weights[None, :], coupling.T, grid, legendre)
 
 
@@ -317,8 +429,18 @@
 
     def shards(grid_data, legendre, gauss_weights, wave_of_slot, first_tile, coupling):
         grid = jnp.transpose(grid_data, (1, 2, 0))
-        back = transform(W, NL, grid, legendre, gauss_weights, wave_of_slot, first_tile, coupling)
-        return jnp.transpose(unpack(wave_of_slot, back), (2, 0, 1))
+        rest = (grid, legendre, gauss_weights, wave_of_slot, first_tile, coupling)
+
+        def everything():
+            return unpack(W, False, wave_of_slot, transform(W, NL, False, *rest)[0])
+
+        if W % 4 or legendre.shape[0] % 2:
+            out = everything()
+        else:
+            back, flag = transform(W, NL, True, *rest)
+            out = lax.cond(
+                flag[0, 0] > 0.5, lambda: unpack(W, True, wave_of_slot, back), everything)
+        return jnp.transpose(out, (2, 0, 1))
 
     placed = (P("wave", None, "lev"), P("wave", None, None), P(), P(), P("wave"), P(None, "lev"))
     return jax.shard_map(

time: 147 us -> 117 us (0.80)
  Pallas kernels: 146 us -> 115 us
    pallas_call x2, Pallas kernels: 146 us -> 115 us  [the longest x1 110 us: transform(): pl.pallas_call(functools.partial(spectral_kernel, W, NL, compact), out_sh...]
where the time goes in v2:
time: 117 us
  Pallas kernels  115 us (98%)
  local copies, waits for them, and re-layouts  1.19 us (1%)
    pallas_call x1, Pallas kernels, transform(): pl.pallas_call(functools.partial(spectral_kernel, W, NL, compact), out_sh...  110 us
    pallas_call x1, Pallas kernels, unpack(): pl.pallas_call(functools.partial(unpack_kernel, W, compact), out_shape=ja...  4.53 us

profile of v2, /device:TPU:0, one launch (start us, length us, event | category | flops | bytes accessed | tf_op | source)
XLA Modules:
  0.0 116.8 jit_solution(4040310455926066665)
XLA Ops:
  0.0 0.0 copy-start
  0.0 0.0 copy-start.1
  0.0 0.0 copy-start.2
  0.0 0.0 copy-start.3
  0.0 110.4 %spectral_half.1 = (f32[32,96,256]{2,1,0:T(8,128)}, f32[8,128]{1,0:T(8,128)}) custom-call(s32[32]{0:T(128)} %wave_ref.1, s32[4]{0:T(128)} %tile_ref.1, f32[1,1024]{1,0:T(1,128)} %bitcast.11, f32[16,64]{1,0:T(8,128)} %bitcast.9, f32[32,96,256]{2,1,0:T(8,128)} %bitcast.7, f32[4,1024,1024]{2,1,0:T(8,128)} %tables_ref.1), custom_call_target="tpu_custom_call" | custom-call | tf_op jit(solution)/shard_map/spectral_half/pallas_call | solution.py:394
  110.4 1.2 %slice.3 = f32[1,1]{1,0:T(1,128)} slice(f32[8,128]{1,0:T(8,128)} %get-tuple-element.35), slice={[0:1], [0:1]} | slice | bytes 8 | tf_op jit(solution)/shard_map/slice | solution.py:442
  112.2 0.0 copy-done
  112.2 0.0 copy-done.1
  112.2 0.0 copy-done.2
  112.2 0.0 copy-done.3
  112.2 4.5 %conditional.1 = (f32[32,96,256]{2,1,0:T(8,128)}) conditional(s32[]{:T(128)} %bitcast.5, (f32[1024]{0:T(1024)S(1)}, f32[64,16]{0,1:T(8,128)S(1)}, s32[32]{0:T(128)S(1)}, s32[4]{0:T(128)S(1)}, f32[32,96,256]{2,1,0:T(8,128)}, /*index=5*/f32[4,1024,1024]{2,1,0:T(8,128)}) %tuple.20, (s32[32]{0:T(128)S(1)}, f32[32,96,256]{2,1,0:T(8,128)}) %tuple.19), branch_computations={%region_0.0_spmd, %region_1.0_spmd} | conditional | bytes 8 | solution.py:441
  112.3 4.5 %unpack_half.1 = f32[32,96,256]{2,1,0:T(8,128)} custom-call(s32[32]{0:T(128)S(1)} %get-tuple-element.31.wave_ref, f32[32,96,256]{2,1,0:T(8,128)} %get-tuple-element.32.y_ref), custom_call_target="tpu_custom_call" | custom-call | tf_op jit(solution)/shard_map/cond/branch_1_fun/unpack_half/pallas_call | solution.py:84
Async XLA Ops:
  0.0 112.2 %copy-start = (f32[64,16]{0,1:T(8,128)S(1)}, f32[64,16]{0,1:T(8,128)}, u32[]{:S(2)}) copy-start(f32[64,16]{0,1:T(8,128)} %param.13) | copy-start | bytes 12292
  0.0 112.2 %copy-start.1 = (f32[1024]{0:T(1024)S(1)}, f32[1024]{0:T(1024)}, u32[]{:S(2)}) copy-start(f32[1024]{0:T(1024)} %param.10) | copy-start | bytes 12292
  0.0 112.2 %copy-start.2 = (s32[32]{0:T(128)S(1)}, s32[32]{0:T(128)}, u32[]{:S(2)}) copy-start(s32[32]{0:T(128)} %wave_ref.1) | copy-start | bytes 388
  0.0 112.2 %copy-start.3 = (s32[4]{0:T(128)S(1)}, s32[4]{0:T(128)}, u32[]{:S(2)}) copy-start(s32[4]{0:T(128)} %tile_ref.1) | copy-start | bytes 52

commit v3 on v2

--- a/solution.py
+++ b/solution.py
@@ -42,41 +42,36 @@
     waves = wave_ref.shape[0]
     halved = polar(lax.axis_index("wave"), W) if compact else False
 
-    def source(s):
-        return jnp.where(halved, s - s % 2, s) if compact else s
-
-    def fetch(s):
-        return pltpu.make_async_copy(y_ref.at[source(s)], held.at[s], in_sem.at[s])
+    group = held.shape[0] // in_sem.shape[0]
+
+    def fetch(g):
+        span = pl.ds(g * group, group)
+        return pltpu.make_async_copy(y_ref.at[span], held.at[span], in_sem.at[g])
 
     def put(s, src):
-        return pltpu.make_async_copy(src, out_ref.at[wave_ref[s]], out_sem.at[s])
-
-    @pl.loop(0, waves)
-    def _(s):
-        fetch(s).start()
-
+        return pltpu.make_async_copy(src, out_ref.at[wave_ref[s]], out_sem)
+
+    for g in range(waves // group):
+        fetch(g).start()
     if compact:
         zero[...] = jnp.zeros_like(zero)
-
-    @pl.loop(0, waves)
-    def _(s):
-        fetch(s).wait()
-        if compact:
-            empty = halved & (wave_ref[s] > wave_ref[s + 1 - 2 * (s % 2)])
-
-            @pl.when(empty)
-            def _():
-                put(s, zero).start()
-
-            @pl.when(jnp.logical_not(empty))
-            def _():
+    for g in range(waves // group):
+        fetch(g).wait()
+        for s in range(g * group, (g + 1) * group):
+            if compact:
+                even = s - s % 2
+                empty = halved & (wave_ref[s] > wave_ref[even + 1 - s % 2])
+
+                @pl.when(empty)
+                def _():
+                    put(s, zero).start()
+
+                @pl.when(jnp.logical_not(empty))
+                def _():
+                    put(s, held.at[jnp.where(halved, even, s)]).start()
+            else:
                 put(s, held.at[s]).start()
-        else:
-            put(s, held.at[s]).start()
-
-    @pl.loop(0, waves)
-    def _(s):
-        put(s, held.at[s]).wait()
+    pltpu.make_async_copy(held, out_ref, out_sem).wait()
 
 
 def unpack(W, compact, wave_of_slot, packed):
@@ -89,8 +84,8 @@
         scratch_shapes=[
             pltpu.VMEM(packed.shape, jnp.float32),
             pltpu.VMEM(packed.shape[1:], jnp.float32),
-            pltpu.SemaphoreType.DMA((waves,)),
-            pltpu.SemaphoreType.DMA((waves,)),
+            pltpu.SemaphoreType.DMA((waves // 4 if waves % 4 == 0 else waves,)),
+            pltpu.SemaphoreType.DMA,
         ],
         compiler_params=pltpu.CompilerParams(vmem_limit_bytes=VMEM_BYTES),
         name="unpack_half" if compact else "unpack",

time: 117 us -> 116 us (level)
    pallas_call x1, Pallas kernels: 4.53 us -> 3.25 us  [unpack(): pl.pallas_call(functools.partial(unpack_kernel, W, compact), out_shape=ja...]
where the time goes in v3:
time: 116 us
  Pallas kernels  114 us (98%)
  local copies, waits for them, and re-layouts  1.19 us (1%)
    pallas_call x1, Pallas kernels, transform(): pl.pallas_call(functools.partial(spectral_kernel, W, NL, compact), out_sh...  110 us
    pallas_call x1, Pallas kernels, unpack(): pl.pallas_call(functools.partial(unpack_kernel, W, compact), out_shape=ja...  3.25 us

profile of v3, /device:TPU:0, one launch (start us, length us, event | category | flops | bytes accessed | tf_op | source)
XLA Modules:
  0.0 115.5 jit_solution(11866124670774434763)
XLA Ops:
  0.0 0.0 copy-start
  0.0 0.0 copy-start.1
  0.0 0.0 copy-start.2
  0.0 0.0 copy-start.3
  0.0 110.4 %spectral_half.1 = (f32[32,96,256]{2,1,0:T(8,128)}, f32[8,128]{1,0:T(8,128)}) custom-call(s32[32]{0:T(128)} %wave_ref.1, s32[4]{0:T(128)} %tile_ref.1, f32[1,1024]{1,0:T(1,128)} %bitcast.11, f32[16,64]{1,0:T(8,128)} %bitcast.9, f32[32,96,256]{2,1,0:T(8,128)} %bitcast.7, f32[4,1024,1024]{2,1,0:T(8,128)} %tables_ref.1), custom_call_target="tpu_custom_call" | custom-call | tf_op jit(solution)/shard_map/spectral_half/pallas_call | solution.py:389
  110.4 1.2 %slice.3 = f32[1,1]{1,0:T(1,128)} slice(f32[8,128]{1,0:T(8,128)} %get-tuple-element.35), slice={[0:1], [0:1]} | slice | bytes 8 | tf_op jit(solution)/shard_map/slice | solution.py:437
  112.2 0.0 copy-done
  112.2 0.0 copy-done.1
  112.2 0.0 copy-done.2
  112.2 0.0 copy-done.3
  112.2 3.3 %conditional.1 = (f32[32,96,256]{2,1,0:T(8,128)}) conditional(s32[]{:T(128)} %bitcast.5, (f32[1024]{0:T(1024)S(1)}, f32[64,16]{0,1:T(8,128)S(1)}, s32[32]{0:T(128)S(1)}, s32[4]{0:T(128)S(1)}, f32[32,96,256]{2,1,0:T(8,128)}, /*index=5*/f32[4,1024,1024]{2,1,0:T(8,128)}) %tuple.20, (s32[32]{0:T(128)S(1)}, f32[32,96,256]{2,1,0:T(8,128)}) %tuple.19), branch_computations={%region_0.0_spmd, %region_1.0_spmd} | conditional | bytes 8 | solution.py:436
  112.3 3.3 %unpack_half.1 = f32[32,96,256]{2,1,0:T(8,128)} custom-call(s32[32]{0:T(128)S(1)} %get-tuple-element.31.wave_ref, f32[32,96,256]{2,1,0:T(8,128)} %get-tuple-element.32.y_ref), custom_call_target="tpu_custom_call" | custom-call | tf_op jit(solution)/shard_map/cond/branch_1_fun/unpack_half/pallas_call | solution.py:79
Async XLA Ops:
  0.0 112.2 %copy-start = (f32[64,16]{0,1:T(8,128)S(1)}, f32[64,16]{0,1:T(8,128)}, u32[]{:S(2)}) copy-start(f32[64,16]{0,1:T(8,128)} %param.13) | copy-start | bytes 12292
  0.0 112.2 %copy-start.1 = (f32[1024]{0:T(1024)S(1)}, f32[1024]{0:T(1024)}, u32[]{:S(2)}) copy-start(f32[1024]{0:T(1024)} %param.10) | copy-start | bytes 12292
  0.0 112.2 %copy-start.2 = (s32[32]{0:T(128)S(1)}, s32[32]{0:T(128)}, u32[]{:S(2)}) copy-start(s32[32]{0:T(128)} %wave_ref.1) | copy-start | bytes 388
  0.0 112.2 %copy-start.3 = (s32[4]{0:T(128)S(1)}, s32[4]{0:T(128)}, u32[]{:S(2)}) copy-start(s32[4]{0:T(128)} %tile_ref.1) | copy-start | bytes 52
